TPU v7x, 128 devices: a whole 4x4x4 slice. The times are simulated.
128 devices in a mesh: grp: 16 (over z, y), tp: 8 (over x, core).
Axes of the slice: x: 4, y: 4, z: 4, core: 2. Of those that a mesh axis runs over, the one named last changes fastest.
Arguments:
- tokens: bfloat16 [1024, 4, 8192], P('grp', None, 'tp'), may hold values from -6 to 6
- adapter_id: int32 [1024], P('grp'), may hold values from 0 to 127, as said below
- pool_slot: int32 [128], replicated, may hold values from 0 to 127, as said below
- lengths: int32 [1024], P('grp'), may hold values from 1 to 64, as said below
- w_query: bfloat16 [8192, 8192], P(None, 'tp'), may hold values from -0.0625 to 0.0625
- w_key: bfloat16 [8192, 1024], P(None, 'tp'), may hold values from -0.0625 to 0.0625
- w_value: bfloat16 [8192, 1024], P(None, 'tp'), may hold values from -0.0625 to 0.0625
- pooled_down_weights: bfloat16 [128, 8192, 64], P('grp', 'tp'), may hold values from -0.0625 to 0.0625
- pool_up: bfloat16 [128, 64, 8192], P('grp', None, 'tp'), may hold values from -0.75 to 0.75
- cache_key: bfloat16 [1024, 64, 1024], P('grp', None, 'tp')
- cache_value: bfloat16 [1024, 64, 1024], P('grp', None, 'tp'), may hold values from -6 to 6
Outputs:
- attended: bfloat16 [1024, 4, 8192], P('grp', None, 'tp')
Inputs may be any that keep to these rules, and one draw needn't show every extreme that they name: `adapter_id`: each aligned block of 64 rows (one group) uses adapters of exactly 8 owners (owner = pool_slot // 8), 8 rows each, and at most 2 distinct adapters of one owner, reached in every block; a single owner, the same for all blocks, serves 8 rows of every block. `pool_slot`: A permutation. `lengths`: each aligned block of 64 rows has a row of length 64.
All inputs are finite; a program needn't handle non-finite values.
Results may differ from a plain program's by a relative error of at most 0.012.
The roundings to bfloat16 on the way count: a program that leaves them out, or rounds other values in their place, can miss the bound.
Values may be sent and summed in bfloat16 or wider, within the bound.
A program may use at most 128 MiB of HBM per device.

v0:
```python
import math
import jax
import jax.numpy as jnp
from jax import lax
from jax.sharding import PartitionSpec as P

HD = 128
CAP = 8
rope_base = 500000.0


def rotate(values, position):
    half_width = values.shape[-1] // 2
    inv_freq = jnp.exp(
        jnp.arange(half_width, dtype=jnp.float32) * (-2.0 * math.log(rope_base) / values.shape[-1])
    )
    angles = position.astype(jnp.float32)[:, :, None, None] * inv_freq
    cosine = jnp.cos(angles)
    sines = jnp.sin(angles)
    front_half = values[..., :half_width]
    back_half = values[..., half_width:]
    return jnp.concatenate(
        [front_half * cosine - back_half * sines, back_half * cosine + front_half * sines], axis=-1
    )


def attend(queries, key_new, value_new, cache_key, cache_value, lengths):
    score_scale = 1.0 / math.sqrt(queries.shape[-1])
    cached = (
        jnp.einsum("rskgd,rlkd->rskgl", queries, cache_key, preferred_element_type=jnp.float32)
        * score_scale
    )
    fresh_scores = (
        jnp.einsum("rskgd,rtkd->rskgt", queries, key_new, preferred_element_type=jnp.float32)
        * score_scale
    )
    live_mask = jnp.arange(cache_key.shape[1], dtype=jnp.int32)[None, :] < lengths[:, None]
    cached = jnp.where(live_mask[:, None, None, None, :], cached, -1e30)
    steps_here = key_new.shape[1]
    causal = (
        jnp.arange(steps_here, dtype=jnp.int32)[:, None]
        >= jnp.arange(steps_here, dtype=jnp.int32)[None, :]
    )
    fresh_scores = jnp.where(causal[None, :, None, None, :], fresh_scores, -1e30)
    row_max = jnp.maximum(jnp.max(cached, axis=-1), jnp.max(fresh_scores, axis=-1))
    cache_exp = jnp.exp(cached - row_max[..., None])
    fresh_exp = jnp.exp(fresh_scores - row_max[..., None])
    weight_sum = jnp.sum(cache_exp, axis=-1) + jnp.sum(fresh_exp, axis=-1)
    cache_weights = (cache_exp / weight_sum[..., None]).astype(jnp.bfloat16)
    fresh_weights = (fresh_exp / weight_sum[..., None]).astype(jnp.bfloat16)
    combined = jnp.einsum(
        "rskgl,rlkd->rskgd", cache_weights, cache_value, preferred_element_type=jnp.float32
    )
    combined = combined + jnp.einsum(
        "rskgt,rtkd->rskgd", fresh_weights, value_new, preferred_element_type=jnp.float32
    )
    return combined.astype(jnp.bfloat16)


def paired_adapter_term(
    tokens_per_block, second_selection, down_weight_pair, up_weight_pair, summing_axis
):
    count_of_blocks, block_length, unused_item = tokens_per_block.shape
    adapter_rank = down_weight_pair.shape[3]
    query_width = up_weight_pair.shape[3]
    selection_mask = jnp.stack([second_selection == 0, second_selection == 1], axis=2)
    partial_value_sum = jnp.einsum(
        "btd,bjdc->btjc", tokens_per_block, down_weight_pair, preferred_element_type=jnp.float32
    )
    partial_value_sum = jnp.sum(
        partial_value_sum * selection_mask[:, :, :, None].astype(jnp.float32), axis=2
    )
    adapter_middle = summing_axis(partial_value_sum).astype(jnp.bfloat16)
    spread_rows = (
        selection_mask[:, :, :, None].astype(jnp.bfloat16) * adapter_middle[:, :, None, :]
    ).reshape(count_of_blocks, block_length, 2 * adapter_rank)
    return jnp.einsum(
        "btk,bkq->btq",
        spread_rows,
        up_weight_pair.reshape(count_of_blocks, 2 * adapter_rank, query_width),
        preferred_element_type=jnp.float32,
    ).astype(jnp.bfloat16)


def body(
    tokens,
    adapter_id,
    pool_slot,
    lengths,
    w_query,
    w_key,
    w_value,
    pooled_down_weights,
    pool_up,
    cache_key,
    cache_value,
):
    group_count = lax.axis_size("grp")
    row_count, step_count, part_width = tokens.shape
    local_adapter_rows, unused_item, adapter_rank = pooled_down_weights.shape
    query_width = w_query.shape[1]
    kv_width = w_key.shape[1]
    kv_local = kv_width // HD
    q_local = query_width // HD
    group_size = q_local // kv_local
    count_of_tokens = row_count * step_count
    adapter_span = jnp.arange(pool_slot.shape[0], dtype=jnp.int32)
    pool_pos = jnp.sum(
        jnp.where(adapter_id[:, None] == adapter_span[None, :], pool_slot[None, :], 0), axis=1
    )
    owner_grp = pool_pos // local_adapter_rows
    local_slot = pool_pos % local_adapter_rows
    owner_span = jnp.arange(group_count, dtype=jnp.int32)
    member = owner_grp[:, None] == owner_span[None, :]
    first_slot = jnp.min(jnp.where(member, local_slot[:, None], local_adapter_rows), axis=0)
    first_slot = jnp.where(first_slot >= local_adapter_rows, 0, first_slot)
    second_slot = jnp.maximum(jnp.max(jnp.where(member, local_slot[:, None], -1), axis=0), 0)
    wanted = jnp.stack([first_slot, second_slot], axis=1)
    asked_slots = lax.all_to_all(wanted, "grp", split_axis=0, concat_axis=0, tiled=True)
    down_weight_panels = pooled_down_weights[asked_slots]
    up_weight_panels = pool_up[asked_slots]
    down_got = lax.all_to_all(down_weight_panels, "grp", split_axis=0, concat_axis=0, tiled=True)
    up_got = lax.all_to_all(up_weight_panels, "grp", split_axis=0, concat_axis=0, tiled=True)
    order = jnp.argsort(owner_grp, stable=True)
    sorted_owner = owner_grp[order]
    count_of_blocks = row_count // CAP
    block_owner = sorted_owner.reshape(count_of_blocks, CAP)[:, 0]
    second_row = (local_slot[order] != first_slot[sorted_owner]).astype(jnp.int32)
    second_tok = jnp.repeat(second_row, step_count).reshape(count_of_blocks, CAP * step_count)
    tokens_per_block = tokens[order].reshape(count_of_blocks, CAP * step_count, part_width)

    def mid_reduce(partial_value_sum):
        return lax.psum(partial_value_sum, "tp")

    sorted_output_rows = paired_adapter_term(
        tokens_per_block, second_tok, down_got[block_owner], up_got[block_owner], mid_reduce
    )
    adapter_output = (
        jnp.zeros((row_count, step_count * query_width), jnp.bfloat16)
        .at[order]
        .set(sorted_output_rows.reshape(row_count, step_count * query_width))
    )
    adapter_output = adapter_output.reshape(count_of_tokens, query_width)
    shard_piece = lax.all_gather(tokens, "tp", axis=2, tiled=True)
    piece_width = shard_piece.shape[2]
    piece_rows = shard_piece.reshape(count_of_tokens, piece_width)

    def add_term(matrix):
        return jnp.dot(piece_rows, matrix, preferred_element_type=jnp.float32)

    base_query_rows = add_term(w_query)
    key_base = add_term(w_key)
    value_base = add_term(w_value)
    base_query_rows = base_query_rows + adapter_output.astype(jnp.float32)
    position = lengths[:, None] + jnp.arange(step_count, dtype=jnp.int32)[None, :]
    queries = rotate(base_query_rows.reshape(row_count, step_count, q_local, HD), position)
    queries = queries.astype(jnp.bfloat16).reshape(row_count, step_count, kv_local, group_size, HD)
    key_new = rotate(key_base.reshape(row_count, step_count, kv_local, HD), position).astype(
        jnp.bfloat16
    )
    value_new = value_base.reshape(row_count, step_count, kv_local, HD).astype(jnp.bfloat16)
    cache_keys = cache_key.reshape(row_count, cache_key.shape[1], kv_local, HD)
    cache_values = cache_value.reshape(row_count, cache_value.shape[1], kv_local, HD)
    combined = attend(queries, key_new, value_new, cache_keys, cache_values, lengths)
    return combined.reshape(row_count, step_count, query_width)


def solution(mesh):
    in_specs = (
        P("grp", None, "tp"),
        P("grp"),
        P(),
        P("grp"),
        P(None, "tp"),
        P(None, "tp"),
        P(None, "tp"),
        P("grp", "tp", None),
        P("grp", None, "tp"),
        P("grp", None, "tp"),
        P("grp", None, "tp"),
    )
    out_specs = P("grp", None, "tp")
    return jax.shard_map(body, mesh=mesh, in_specs=in_specs, out_specs=out_specs, check_vma=False)
```

profile of v0, /device:TPU:0, one launch (start us, length us, event | category | flops | bytes accessed | tf_op | source)
XLA Modules:
  0.0 206.0 jit_solution(8176694837420051661)
XLA Ops:
  6.5 1.0 select_reduce_fusion
  7.8 15.5 %all_to_all.22 = s32[16,1,2]{2,1,0:T(1,128)S(1)} all-to-all(s32[16,1,2]{2,1,0:T(1,128)S(1)} %copy.47), channel_id=1, replica_groups=mesh['grp'=16,'tp'=8] {'grp'}, dimensions={0} | all-to-all | bytes 256 | tf_op jit(solution)/shard_map/all_to_all | solution.py:119
  23.6 4.0 %gather_fusion.4 = bf16[32,1024,64]{1,2,0:T(8,128)(2,1)} fusion(bf16[8,1024,64]{1,2,0:T(8,128)(2,1)} %param.18, s32[1024]{0:T(1024)S(1)} %pad_clamp_fusion.1), kind=kCustom, calls=%fused_computation.4 | custom fusion | bytes 8388736 | tf_op jit(solution)/shard_map/gather | solution.py:120
  27.6 4.7 %all-to-all-start.1 = ((bf16[16,2,1024,64]{2,3,1,0:T(8,128)(2,1)}), bf16[16,2,1024,64]{2,3,1,0:T(8,128)(2,1)}, u32[]{:S(2)}, u32[]{:S(2)}) async-start(bf16[16,2,1024,64]{2,3,1,0:T(8,128)(2,1)} %bitcast.99), calls=%async_computation.1 | async-start | bytes 8388608 | tf_op jit(solution)/shard_map/all_to_all | solution.py:122
  32.3 2.0 copy.40
  34.3 2.8 %gather_fusion.6 = bf16[32,64,1024]{2,1,0:T(8,128)(2,1)} fusion(bf16[8,64,1024]{2,1,0:T(8,128)(2,1)S(1)} %copy-done.2, s32[1024]{0:T(1024)S(1)} %pad_clamp_fusion.1), kind=kCustom, calls=%fused_computation.6 | custom fusion | bytes 8388736 | tf_op jit(solution)/shard_map/gather | solution.py:121
  37.1 55.2 %all-to-all-done.1 = bf16[16,2,1024,64]{2,3,1,0:T(8,128)(2,1)} async-done(((bf16[16,2,1024,64]{2,3,1,0:T(8,128)(2,1)}), bf16[16,2,1024,64]{2,3,1,0:T(8,128)(2,1)}, u32[]{:S(2)}, u32[]{:S(2)}) %all-to-all-start.1) | async-done | bytes 4194336 | tf_op jit(solution)/shard_map/all_to_all | solution.py:122
  92.3 4.7 %all-to-all-start.2 = ((bf16[16,2,64,1024]{3,2,1,0:T(8,128)(2,1)}), bf16[16,2,64,1024]{3,2,1,0:T(8,128)(2,1)}, u32[]{:S(2)}, u32[]{:S(2)}) async-start(bf16[16,2,64,1024]{3,2,1,0:T(8,128)(2,1)} %bitcast.100), calls=%async_computation.2 | async-start | bytes 8388608 | tf_op jit(solution)/shard_map/all_to_all | solution.py:123
  97.0 2.0 sort.17
  99.0 0.8 gather_fusion.1
  99.8 0.8 gather_fusion
  100.6 1.0 gather_fusion.3
  101.7 0.8 gather_fusion.2
  103.7 1.1 multiply_cosine_fusion.1
  104.8 4.2 %gather_fusion.5 = bf16[8,2,1024,64]{2,3,1,0:T(8,128)(2,1)} fusion(bf16[16,2,1024,64]{2,3,1,0:T(8,128)(2,1)} %all-to-all-done.1, s32[1024]{0:T(1024)S(1)} %pad_clamp_fusion), kind=kCustom, calls=%fused_computation.5 | custom fusion | bytes 4194336 | tf_op jit(solution)/shard_map/gather | solution.py:136
  109.0 2.7 %fusion.11 = f32[8,32,64]{2,1,0:T(8,128)S(1)} fusion(bf16[8,2,1024,64]{2,3,1,0:T(8,128)(2,1)} %gather_fusion.5, bf16[8,32,1024,1]{2,1,0,3:T(8,128)(2,1)S(1)} %reshape.452, f32[8,32,2]{1,2,0:T(2,128)S(1)} %copy.50), kind=kOutput, calls=%fused_computation.27 | convolution fusion | flops 67158016 | bytes 2689024 | tf_op jit(solution)/shard_map/btd,bjdc->btjc/dot_general | solution.py:67
  111.7 26.3 %psum.7 = bf16[8,32,64]{2,1,0:T(8,128)(2,1)S(1)} all-reduce(f32[8,32,64]{2,1,0:T(8,128)S(1)} %fusion.11), channel_id=1, replica_groups=mesh['grp'=16,'tp'=8] {'tp'}, use_global_device_ids=true, to_apply=%region_5.6 | all-reduce | flops 16384 | bytes 98304 | tf_op jit(solution)/shard_map/psum | solution.py:133
  138.5 15.7 %all-to-all-done.2 = bf16[16,2,64,1024]{3,2,1,0:T(8,128)(2,1)} async-done(((bf16[16,2,64,1024]{3,2,1,0:T(8,128)(2,1)}), bf16[16,2,64,1024]{3,2,1,0:T(8,128)(2,1)}, u32[]{:S(2)}, u32[]{:S(2)}) %all-to-all-start.2) | async-done | bytes 4194336 | tf_op jit(solution)/shard_map/all_to_all | solution.py:123
  154.1 4.2 %gather_fusion.7 = bf16[8,2,64,1024]{3,2,1,0:T(8,128)(2,1)} fusion(bf16[16,2,64,1024]{3,2,1,0:T(8,128)(2,1)} %all-to-all-done.2, s32[1024]{0:T(1024)S(1)} %pad_clamp_fusion), kind=kCustom, calls=%fused_computation.7 | custom fusion | bytes 4194336 | tf_op jit(solution)/shard_map/gather | solution.py:136
  158.3 2.0 convolution_convert_fusion
  160.6 1.5 scatter_custom_fusion
  162.1 1.3 reshape.373
  163.4 7.4 %copy.41 = bf16[64,4,8192]{2,1,0:T(4,128)(2,1)} copy(bf16[64,4,8192]{2,0,1:T(8,128)(2,1)} %all-gather.2.cloned.1.call-done) | data formatting | bytes 8388608 | tf_op jit(solution)/shard_map/all_gather | solution.py:144
  170.8 7.0 %reshape.364 = bf16[256,8192]{1,0:T(8,128)(2,1)} reshape(bf16[64,4,8192]{2,1,0:T(4,128)(2,1)} %copy.41) | data formatting | bytes 8388608 | tf_op jit(solution)/shard_map/reshape | solution.py:146
  177.8 9.5 %fusion.4 = f32[32,8,8,128]{3,1,2,0:T(8,128)S(1)} fusion(f32[256,1024]{1,0:T(8,128)S(1)} %copy-done.6, bf16[256,8192]{1,0:T(8,128)(2,1)} %reshape.364, bf16[8192,1024]{1,0:T(8,128)(2,1)} %param.15), kind=kOutput, calls=%fused_computation.14 | convolution fusion | flops 4295229440 | bytes 23068672 | tf_op jit(solution)/shard_map/dot_general | solution.py:149
  187.5 1.3 fusion.12
  190.1 2.6 %fusion.52 = (f32[64,4,8]{2,1,0:T(4,128)S(1)}, f32[64,4,1,8,4]{3,4,1,0,2:T(4,128)S(1)}) fusion(bf16[64,4,8,64]{3,2,1,0:T(8,128)(2,1)S(1)} %get-tuple-element.10, bf16[64,4,8,64]{3,2,1,0:T(8,128)(2,1)S(1)} %get-tuple-element.9, bf16[64,4,128,1]{2,0,1,3:T(8,128)(2,1)S(1)} %maximum_bitcast_fusion, pred[4,4]{1,0:T(4,128)(4,1)S(1)} %iota_compare_fusion.3), kind=kOutput, calls=%fused_computation.105 | convolution fusion | flops 3168256 | bytes 630800 | tf_op jit(solution)/shard_map/rskgd,rtkd->rskgt/dot_general | solution.py:34
  192.7 0.9 fusion.51
  194.1 0.8 fusion.24
  194.9 0.9 convolution_bitcast_fusion
  196.4 1.3 fusion.18
  198.2 0.9 reshape.372
  (70 shorter events, 5.7 us)
Async XLA Ops:
  6.5 181.0 %copy-start = (bf16[8192,128]{1,0:T(8,128)(2,1)S(1)}, bf16[8192,128]{1,0:T(8,128)(2,1)}, u32[]{:S(2)}) copy-start(bf16[8192,128]{1,0:T(8,128)(2,1)} %param.16) | copy-start | bytes 6291460
  27.6 6.7 %copy-start.2 = (bf16[8,64,1024]{2,1,0:T(8,128)(2,1)S(1)}, bf16[8,64,1024]{2,1,0:T(8,128)(2,1)}, u32[]{:S(2)}) copy-start(bf16[8,64,1024]{2,1,0:T(8,128)(2,1)} %param.19) | copy-start | bytes 3145732
  27.6 64.7 %all-to-all-start.1 = ((bf16[16,2,1024,64]{2,3,1,0:T(8,128)(2,1)}), bf16[16,2,1024,64]{2,3,1,0:T(8,128)(2,1)}, u32[]{:S(2)}, u32[]{:S(2)}) async-start(bf16[16,2,1024,64]{2,3,1,0:T(8,128)(2,1)} %bitcast.99), calls=%async_computation.1 | async-start | bytes 8388608 | tf_op jit(solution)/shard_map/all_to_all | solution.py:122
  32.2 131.2 %all-gather.2.cloned.1.call-start = ((), (), s32[]{:S(2)}) async-start(), calls=%async_computation.3 | async-start | bytes 4718592 | tf_op jit(solution)/shard_map/all_gather | solution.py:144
  92.3 8.3 %copy-start.4 = (bf16[64,4,1024]{2,1,0:T(4,128)(2,1)S(1)}, bf16[64,4,1024]{2,1,0:T(4,128)(2,1)}, u32[]{:S(2)}) copy-start(bf16[64,4,1024]{2,1,0:T(4,128)(2,1)} %param.11) | copy-start | bytes 1572868
  92.3 11.1 %copy-start.7 = (s32[64]{0:T(128)S(1)}, s32[64]{0:T(128)}, u32[]{:S(2)}) copy-start(s32[64]{0:T(128)} %param.14) | copy-start | bytes 772
  92.3 61.8 %all-to-all-start.2 = ((bf16[16,2,64,1024]{3,2,1,0:T(8,128)(2,1)}), bf16[16,2,64,1024]{3,2,1,0:T(8,128)(2,1)}, u32[]{:S(2)}, u32[]{:S(2)}) async-start(bf16[16,2,64,1024]{3,2,1,0:T(8,128)(2,1)} %bitcast.100), calls=%async_computation.2 | async-start | bytes 8388608 | tf_op jit(solution)/shard_map/all_to_all | solution.py:123
  170.8 7.0 %copy-start.6 = (f32[256,1024]{1,0:T(8,128)S(1)}, f32[256,1024]{1,0:T(8,128)}, u32[]{:S(2)}) copy-start(f32[256,1024]{1,0:T(8,128)} %reshape.373) | copy-start | bytes 3145732
  177.8 9.7 %copy-start.1 = (bf16[64,4,8192]{2,0,1:T(8,128)(2,1)S(1)}, bf16[64,4,8192]{2,0,1:T(8,128)(2,1)}, u32[]{:S(2)}) copy-start(bf16[64,4,8192]{2,0,1:T(8,128)(2,1)} %all-gather.2.cloned.1.call-done) | copy-start | bytes 12582916
  188.9 3.8 %copy-start.5 = (bf16[64,64,128]{2,1,0:T(8,128)(2,1)S(1)}, bf16[64,64,128]{2,1,0:T(8,128)(2,1)}, u32[]{:S(2)}) copy-start(bf16[64,64,128]{2,1,0:T(8,128)(2,1)} %param.20) | copy-start | bytes 3145732
  190.1 4.8 %copy-start.8 = (bf16[64,64,128]{2,1,0:T(8,128)(2,1)S(1)}, bf16[64,64,128]{2,1,0:T(8,128)(2,1)}, u32[]{:S(2)}) copy-start(bf16[64,64,128]{2,1,0:T(8,128)(2,1)} %param.21) | copy-start | bytes 3145732
  194.8 1.6 copy-start.3
Sparse Core Ops, SparseCore 0:
  34.8 33.4 all-gather.1
where the time goes:
time: 207 us; the launch traced here: 206 us
  waiting for transfers between devices  70.9 us (34%)
  blocking collectives  41.8 us (20%)
  local copies, waits for them, and re-layouts  41.2 us (20%)
  matrix products  21.6 us (10%)
  between operations  13.7 us (7%)
  starting transfers between devices  9.38 us (5%)
  other arithmetic  7.4 us (4%)
    all_to_all x1, waiting for transfers between devices, body(): lax.all_to_all(down_weight_panels, 'grp', split_axis=0, concat_axis=0, ti...  55.2 us
    psum x1, blocking collectives, mid_reduce(): return lax.psum(partial_value_sum, 'tp')  26.3 us
    all_to_all x1, waiting for transfers between devices, body(): lax.all_to_all(up_weight_panels, 'grp', split_axis=0, concat_axis=0, tile...  15.7 us
    all_to_all x1, blocking collectives, body(): lax.all_to_all(wanted, 'grp', split_axis=0, concat_axis=0, tiled=True)  15.5 us
    dot_general x3, matrix products, add_term(): return jnp.dot(piece_rows, matrix, preferred_element_type=jnp.float32)  12.1 us
    all_gather x1, local copies, waits for them, and re-layouts, body(): shard_piece = lax.all_gather(tokens, 'tp', axis=2, tiled=True)  7.4 us
    reshape x1, local copies, waits for them, and re-layouts, body(): piece_rows = shard_piece.reshape(count_of_tokens, piece_width)  6.99 us
    all_to_all x1, starting transfers between devices, body(): lax.all_to_all(up_weight_panels, 'grp', split_axis=0, concat_axis=0, tile...  4.68 us
  transfers between devices with their start and end apart: 3, of which 2 were waited for; matrix products, arithmetic and copies ran while one was open for 14% of the time, Pallas kernels for 0%

commit v1 on v0

--- a/solution.py
+++ b/solution.py
@@ -7,6 +7,12 @@
 HD = 128
 CAP = 8
 rope_base = 500000.0
+
+
+def joined_along(blocks, dim):
+    blocks = jnp.moveaxis(blocks, 0, dim)
+    shape = blocks.shape
+    return blocks.reshape(*shape[:dim], shape[dim] * shape[dim + 1], *shape[dim + 2 :])
 
 
 def rotate(values, position):
@@ -141,7 +147,19 @@
         .set(sorted_output_rows.reshape(row_count, step_count * query_width))
     )
     adapter_output = adapter_output.reshape(count_of_tokens, query_width)
-    shard_piece = lax.all_gather(tokens, "tp", axis=2, tiled=True)
+    length = lax.axis_size("tp")
+    pairs = [(i, (i + 1) % length) for i in range(length)]
+    back = [(b, a) for a, b in pairs]
+    lower, upper = ([], [])
+    for turn in range(length - 1):
+        if turn % 2 == 0:
+            lower.append(lax.ppermute(lower[-1] if lower else tokens, "tp", pairs))
+        else:
+            upper.append(lax.ppermute(upper[-1] if upper else tokens, "tp", back))
+    pieces = jnp.stack([*lower[::-1], tokens, *upper])
+    shift = lax.axis_index("tp") - len(lower)
+    pieces = pieces[(jnp.arange(length) - shift) % length]
+    shard_piece = joined_along(pieces, 2)
     piece_width = shard_piece.shape[2]
     piece_rows = shard_piece.reshape(count_of_tokens, piece_width)
 

time: 207 us -> 200 us (0.966)
  local copies, waits for them, and re-layouts: 41.2 us -> 71.3 us
  waiting for transfers between devices: 70.9 us -> 47.8 us
  blocking collectives: 41.8 us -> 27.5 us
  starting transfers between devices: 9.38 us -> 23.3 us
  between operations: 13.7 us -> 0.45 us
    all_to_all x1, waiting for transfers between devices: 55.2 us -> 26.1 us  [body(): lax.all_to_all(down_weight_panels, 'grp', split_axis=0, concat_axis=0, ti...]
    ppermute x0 -> x7, waiting for transfers between devices: none -> 17.2 us  [the longest x4 17.2 us: body(): lower.append(lax.ppermute(lower[-1] if lower else tokens, 'tp', pairs))]
    unnamed x20 -> x31, local copies, waits for them, and re-layouts: 2.82 us -> 19.7 us
    all_to_all x1, waiting for transfers between devices: 15.7 us -> 0.01 us  [body(): lax.all_to_all(up_weight_panels, 'grp', split_axis=0, concat_axis=0, tile...]
    all_to_all x1 -> x0, blocking collectives: 15.5 us -> none  [body(): lax.all_to_all(wanted, 'grp', split_axis=0, concat_axis=0, tiled=True)]
    transpose x0 -> x2, local copies, waits for them, and re-layouts: none -> 11 us  [joined_along(): blocks = jnp.moveaxis(blocks, 0, dim)]
    all_to_all x0 -> x1, starting transfers between devices: none -> 8.13 us  [body(): lax.all_to_all(wanted, 'grp', split_axis=0, concat_axis=0, tiled=True)]
    gather x0 -> x1, local copies, waits for them, and re-layouts: none -> 7.52 us  [body(): pieces = pieces[(jnp.arange(length) - shift) % length]]
  transfers between devices with their start and end apart: 3 -> 10, of which waited for: 2 -> 5; matrix products, arithmetic and copies ran while one was open for 14% -> 36% of each run, Pallas kernels for 0% -> 0%
where the time goes in v1:
time: 200 us; the launch traced here: 199 us
  local copies, waits for them, and re-layouts  71.3 us (36%)
  waiting for transfers between devices  47.8 us (24%)
  blocking collectives  27.5 us (14%)
  starting transfers between devices  23.3 us (12%)
  matrix products  21 us (10%)
  other arithmetic  7.62 us (4%)
    psum x1, blocking collectives, mid_reduce(): return lax.psum(partial_value_sum, 'tp')  27.5 us
    all_to_all x1, waiting for transfers between devices, body(): lax.all_to_all(down_weight_panels, 'grp', split_axis=0, concat_axis=0, ti...  26.1 us
    unnamed x31, local copies, waits for them, and re-layouts  19.7 us
    ppermute x4, waiting for transfers between devices, body(): lower.append(lax.ppermute(lower[-1] if lower else tokens, 'tp', pairs))  17.2 us
    dot_general x3, matrix products, add_term(): return jnp.dot(piece_rows, matrix, preferred_element_type=jnp.float32)  14.6 us
    transpose x2, local copies, waits for them, and re-layouts, joined_along(): blocks = jnp.moveaxis(blocks, 0, dim)  11 us
    all_to_all x1, starting transfers between devices, body(): lax.all_to_all(wanted, 'grp', split_axis=0, concat_axis=0, tiled=True)  8.13 us
    gather x1, local copies, waits for them, and re-layouts, body(): pieces = pieces[(jnp.arange(length) - shift) % length]  7.52 us
  transfers between devices with their start and end apart: 10, of which 5 were waited for; matrix products, arithmetic and copies ran while one was open for 36% of the time, Pallas kernels for 0%

profile of v1, /device:TPU:0, one launch (start us, length us, event | category | flops | bytes accessed | tf_op | source)
XLA Modules:
  0.0 199.0 jit_solution(15174246949574372158)
XLA Ops:
  1.9 8.1 %all-to-all-start = ((s32[16,1,2]{2,1,0:T(1,128)}), s32[16,1,2]{2,1,0:T(1,128)S(1)}, u32[]{:S(2)}, u32[]{:S(2)}) async-start(s32[16,1,2]{2,1,0:T(1,128)} %copy.45), calls=%async_computation | async-start | bytes 16384 | tf_op jit(solution)/shard_map/all_to_all | solution.py:125
  10.0 2.1 %sort.17 = (s32[64]{0:T(128)}, s32[64]{0:T(128)S(1)}) sort(s32[64]{0:T(128)S(1)} %get-tuple-element.20, s32[64]{0:T(128)S(1)} %iota.52), dimensions={0}, to_apply=%region_1.2 | sort | flops 384 | bytes 1024 | tf_op jit(solution)/shard_map/jit(argsort)/sort | solution.py:130
  12.9 4.6 %all-to-all-done = s32[16,1,2]{2,1,0:T(1,128)S(1)} async-done(((s32[16,1,2]{2,1,0:T(1,128)}), s32[16,1,2]{2,1,0:T(1,128)S(1)}, u32[]{:S(2)}, u32[]{:S(2)}) %all-to-all-start) | async-done | bytes 160 | tf_op jit(solution)/shard_map/all_to_all | solution.py:125
  17.8 4.0 %gather_fusion.5 = bf16[32,1024,64]{1,2,0:T(8,128)(2,1)} fusion(bf16[8,1024,64]{1,2,0:T(8,128)(2,1)} %param.18, s32[1024]{0:T(1024)S(1)} %get-tuple-element.25), kind=kCustom, calls=%fused_computation.5 | custom fusion | bytes 8388736 | tf_op jit(solution)/shard_map/gather | solution.py:126
  21.8 4.7 %all-to-all-start.1 = ((bf16[16,2,1024,64]{2,3,1,0:T(8,128)(2,1)}), bf16[16,2,1024,64]{2,3,1,0:T(8,128)(2,1)}, u32[]{:S(2)}, u32[]{:S(2)}) async-start(bf16[16,2,1024,64]{2,3,1,0:T(8,128)(2,1)} %bitcast.125), calls=%async_computation.1 | async-start | bytes 8388608 | tf_op jit(solution)/shard_map/all_to_all | solution.py:128
  26.5 2.9 %collective-permute-start.4 = (bf16[64,4,1024]{2,1,0:T(4,128)(2,1)}, bf16[64,4,1024]{2,1,0:T(4,128)(2,1)}, u32[]{:S(2)}, u32[]{:S(2)}) collective-permute-start(bf16[64,4,1024]{2,1,0:T(4,128)(2,1)} %param.11), channel_id=1, source_target_pairs={{1,0},{2,1},{3,2},{4,3},{5,4},{6,5},{7,6},{0,7},{9,8},{10,9},{11,1... | collective-permute-start | bytes 1572872 | tf_op jit(solution)/shard_map/ppermute | solution.py:158
  29.4 7.2 %collective-permute-done = bf16[64,4,1024]{2,1,0:T(4,128)(2,1)} collective-permute-done((bf16[64,4,1024]{2,1,0:T(4,128)(2,1)}, bf16[64,4,1024]{2,1,0:T(4,128)(2,1)}, u32[]{:S(2)}, u32[]{:S(2)}) %collective-permute-start) | collective-permute-done | bytes 524320 | tf_op jit(solution)/shard_map/ppermute | solution.py:156
  37.5 2.8 %gather_fusion.4 = bf16[64,4,1024]{2,1,0:T(4,128)(2,1)} fusion(bf16[64,4,1024]{2,1,0:T(4,128)(2,1)} %param.11, s32[1024]{0:T(1024)S(1)} %pad_clamp_fusion.3), kind=kCustom, calls=%fused_computation.4 | custom fusion | bytes 1048832 | tf_op jit(solution)/shard_map/gather | solution.py:136
  40.3 2.0 %reshape.505 = bf16[8,32,1024,1]{2,1,0,3:T(8,128)(2,1)} reshape(bf16[64,4,1024]{2,1,0:T(4,128)(2,1)} %gather_fusion.4) | data formatting | bytes 1048576 | tf_op jit(solution)/shard_map/reshape | solution.py:136
  42.7 4.1 %collective-permute-done.1 = bf16[64,4,1024]{2,1,0:T(4,128)(2,1)} collective-permute-done((bf16[64,4,1024]{2,1,0:T(4,128)(2,1)}, bf16[64,4,1024]{2,1,0:T(4,128)(2,1)}, u32[]{:S(2)}, u32[]{:S(2)}) %collective-permute-start.1) | collective-permute-done | bytes 524320 | tf_op jit(solution)/shard_map/ppermute | solution.py:156
  47.9 3.0 %collective-permute-start.5 = (bf16[64,4,1024]{2,1,0:T(4,128)(2,1)}, bf16[64,4,1024]{2,1,0:T(4,128)(2,1)}, u32[]{:S(2)}, u32[]{:S(2)}) collective-permute-start(bf16[64,4,1024]{2,1,0:T(4,128)(2,1)} %collective-permute-done.4), channel_id=1, source_target_pairs={{1,0},{2,1},{3,2},{4,3},{5,4},{6,5},{7,6},{0,7},{9,8},{10,9},{11,1... | collective-permute-start | bytes 1572872 | tf_op jit(solution)/shard_map/ppermute | solution.py:158
  50.9 6.0 %collective-permute-done.2 = bf16[64,4,1024]{2,1,0:T(4,128)(2,1)} collective-permute-done((bf16[64,4,1024]{2,1,0:T(4,128)(2,1)}, bf16[64,4,1024]{2,1,0:T(4,128)(2,1)}, u32[]{:S(2)}, u32[]{:S(2)}) %collective-permute-start.2) | collective-permute-done | bytes 524320 | tf_op jit(solution)/shard_map/ppermute | solution.py:156
  56.9 2.8 %gather_fusion.7 = bf16[32,64,1024]{2,1,0:T(8,128)(2,1)} fusion(bf16[8,64,1024]{2,1,0:T(8,128)(2,1)S(1)} %copy-done.4, s32[1024]{0:T(1024)S(1)} %get-tuple-element.25), kind=kCustom, calls=%fused_computation.7 | custom fusion | bytes 8388736 | tf_op jit(solution)/shard_map/gather | solution.py:127
  60.4 26.1 %all-to-all-done.1 = bf16[16,2,1024,64]{2,3,1,0:T(8,128)(2,1)} async-done(((bf16[16,2,1024,64]{2,3,1,0:T(8,128)(2,1)}), bf16[16,2,1024,64]{2,3,1,0:T(8,128)(2,1)}, u32[]{:S(2)}, u32[]{:S(2)}) %all-to-all-start.1) | async-done | bytes 4194336 | tf_op jit(solution)/shard_map/all_to_all | solution.py:128
  86.5 4.5 %all-to-all-start.2 = ((bf16[16,2,64,1024]{3,2,1,0:T(8,128)(2,1)}), bf16[16,2,64,1024]{3,2,1,0:T(8,128)(2,1)}, u32[]{:S(2)}, u32[]{:S(2)}) async-start(bf16[16,2,64,1024]{3,2,1,0:T(8,128)(2,1)} %bitcast.126), calls=%async_computation.2 | async-start | bytes 8388608 | tf_op jit(solution)/shard_map/all_to_all | solution.py:129
  91.8 2.0 %bitcast_dynamic-update-slice_fusion.7 = bf16[8,64,4,1024]{3,2,1,0:T(4,128)(2,1)} fusion(bf16[64,4,1024]{2,1,0:T(4,128)(2,1)} %collective-permute-done.3), kind=kLoop, calls=%fused_computation.50 | loop fusion | bytes 1048576
  93.9 2.1 %bitcast_dynamic-update-slice_fusion.6 = bf16[8,64,4,1024]{3,2,1,0:T(4,128)(2,1)} fusion(bf16[8,64,4,1024]{3,2,1,0:T(4,128)(2,1)} %bitcast_dynamic-update-slice_fusion.7, bf16[64,4,1024]{2,1,0:T(4,128)(2,1)} %collective-permute-done.2), kind=kLoop, calls=%fused_computation.49 | loop fusion | bytes 1048576
  96.0 2.0 %bitcast_dynamic-update-slice_fusion.5 = bf16[8,64,4,1024]{3,2,1,0:T(4,128)(2,1)} fusion(bf16[8,64,4,1024]{3,2,1,0:T(4,128)(2,1)} %bitcast_dynamic-update-slice_fusion.6, bf16[64,4,1024]{2,1,0:T(4,128)(2,1)} %collective-permute-done.1), kind=kLoop, calls=%fused_computation.48 | loop fusion | bytes 1048576
  98.0 2.0 %bitcast_dynamic-update-slice_fusion.4 = bf16[8,64,4,1024]{3,2,1,0:T(4,128)(2,1)} fusion(bf16[8,64,4,1024]{3,2,1,0:T(4,128)(2,1)} %bitcast_dynamic-update-slice_fusion.5, bf16[64,4,1024]{2,1,0:T(4,128)(2,1)} %collective-permute-done), kind=kLoop, calls=%fused_computation.47 | loop fusion | bytes 1048576
  101.0 2.0 %bitcast_dynamic-update-slice_fusion.2 = bf16[8,64,4,1024]{3,2,1,0:T(4,128)(2,1)} fusion(bf16[8,64,4,1024]{3,2,1,0:T(4,128)(2,1)} %bitcast_dynamic-update-slice_fusion.3, bf16[64,4,1024]{2,1,0:T(4,128)(2,1)} %collective-permute-done.4), kind=kLoop, calls=%fused_computation.45 | loop fusion | bytes 1048576
  103.0 2.0 %bitcast_dynamic-update-slice_fusion.1 = bf16[8,64,4,1024]{3,2,1,0:T(4,128)(2,1)} fusion(bf16[8,64,4,1024]{3,2,1,0:T(4,128)(2,1)} %bitcast_dynamic-update-slice_fusion.2, bf16[64,4,1024]{2,1,0:T(4,128)(2,1)} %collective-permute-done.5), kind=kLoop, calls=%fused_computation.44 | loop fusion | bytes 1048576
  106.0 7.5 %gather_fusion = bf16[8,64,4,1024]{3,2,1,0:T(4,128)(2,1)} fusion(bf16[8,64,4,1024]{3,2,1,0:T(4,128)(2,1)} %bitcast_dynamic-update-slice_fusion, s32[1024]{0:T(1024)S(1)} %pad_clamp_fusion.4), kind=kCustom, calls=%fused_computation | custom fusion | bytes 8388640 | tf_op jit(solution)/shard_map/gather | solution.py:161
  113.5 6.8 %copy.39 = bf16[64,4,8,1024]{3,2,1,0:T(8,128)(2,1)S(1)} copy(bf16[64,4,8,1024]{3,1,0,2:T(4,128)(2,1)} %bitcast.123) | data formatting | bytes 8388608 | tf_op jit(solution)/shard_map/transpose | solution.py:13
  120.3 4.3 %copy.50 = bf16[64,4,8,1024]{3,2,0,1:T(8,128)(2,1)} copy(bf16[64,4,8,1024]{3,1,0,2:T(4,128)(2,1)S(1)} %bitcast.124) | data formatting | bytes 8388608 | tf_op jit(solution)/shard_map/transpose | solution.py:13
  124.6 6.3 %copy.62 = bf16[32,8,8,1024]{3,1,2,0:T(8,128)(2,1)} copy(bf16[32,8,8,1024]{3,2,1,0:T(8,128)(2,1)S(1)} %bitcast.127) | data formatting | bytes 8388608
  130.9 7.4 %dot_general.37 = bf16[64,4,8192]{2,0,1:T(8,128)(2,1)} reshape(bf16[64,4,8,1024]{3,2,0,1:T(8,128)(2,1)} %copy.50) | data formatting | bytes 8388608 | tf_op jit(solution)/shard_map/dot_general | solution.py:167
  138.3 3.6 %fusion.12 = f32[64,4,1,128]{3,0,1,2:T(8,128)S(1)} fusion(bf16[64,4,8192]{2,0,1:T(8,128)(2,1)} %dot_general.37, bf16[8192,128]{1,0:T(8,128)(2,1)S(1)} %copy-done), kind=kOutput, calls=%fused_computation.29 | convolution fusion | flops 536870912 | bytes 6422528 | tf_op jit(solution)/shard_map/dot_general | solution.py:167
  143.9 2.9 %gather_fusion.6 = bf16[8,2,1024,64]{2,3,1,0:T(8,128)(2,1)S(1)} fusion(bf16[16,2,1024,64]{2,3,1,0:T(8,128)(2,1)} %all-to-all-done.1, s32[1024]{0:T(1024)S(1)} %pad_clamp_fusion), kind=kCustom, calls=%fused_computation.6 | custom fusion | bytes 4194336 | tf_op jit(solution)/shard_map/gather | solution.py:142
  147.9 27.5 %psum.7 = bf16[8,32,64]{2,1,0:T(8,128)(2,1)S(1)} all-reduce(f32[8,32,64]{2,1,0:T(8,128)S(1)} %fusion.11), channel_id=1, replica_groups=mesh['grp'=16,'tp'=8] {'tp'}, use_global_device_ids=true, to_apply=%region_5.6 | all-reduce | flops 16384 | bytes 98304 | tf_op jit(solution)/shard_map/psum | solution.py:139
  175.9 2.9 %gather_fusion.8 = bf16[8,2,64,1024]{3,2,1,0:T(8,128)(2,1)S(1)} fusion(bf16[16,2,64,1024]{3,2,1,0:T(8,128)(2,1)} %all-to-all-done.2, s32[1024]{0:T(1024)S(1)} %pad_clamp_fusion), kind=kCustom, calls=%fused_computation.8 | custom fusion | bytes 4194336 | tf_op jit(solution)/shard_map/gather | solution.py:142
  181.3 9.7 %fusion.4 = f32[32,8,8,128]{3,1,2,0:T(8,128)S(1)} fusion(f32[256,1024]{1,0:T(8,128)S(1)} %reshape.418, bf16[256,8192]{1,0:T(8,128)(2,1)} %bitcast.130, bf16[8192,1024]{1,0:T(8,128)(2,1)} %param.15), kind=kOutput, calls=%fused_computation.15 | convolution fusion | flops 4295229440 | bytes 23068672 | tf_op jit(solution)/shard_map/dot_general | solution.py:167
  191.8 2.6 %fusion.57 = (f32[64,4,8]{2,1,0:T(4,128)S(1)}, f32[64,4,1,8,4]{3,4,1,0,2:T(4,128)S(1)}) fusion(bf16[64,4,8,64]{3,2,1,0:T(8,128)(2,1)S(1)} %get-tuple-element.10, bf16[64,4,8,64]{3,2,1,0:T(8,128)(2,1)S(1)} %get-tuple-element.9, bf16[64,4,128,1]{2,0,1,3:T(8,128)(2,1)S(1)} %maximum_bitcast_fusion, pred[4,4]{1,0:T(4,128)(4,1)S(1)} %iota_compare_fusion.3), kind=kOutput, calls=%fused_computation.124 | convolution fusion | flops 3168256 | bytes 630800 | tf_op jit(solution)/shard_map/rskgd,rtkd->rskgt/dot_general | solution.py:40
  (97 shorter events, 20.0 us)
Async XLA Ops:
  0.0 138.3 %copy-start = (bf16[8192,128]{1,0:T(8,128)(2,1)S(1)}, bf16[8192,128]{1,0:T(8,128)(2,1)}, u32[]{:S(2)}) copy-start(bf16[8192,128]{1,0:T(8,128)(2,1)} %param.16) | copy-start | bytes 6291460
  1.9 15.6 %all-to-all-start = ((s32[16,1,2]{2,1,0:T(1,128)}), s32[16,1,2]{2,1,0:T(1,128)S(1)}, u32[]{:S(2)}, u32[]{:S(2)}) async-start(s32[16,1,2]{2,1,0:T(1,128)} %copy.45), calls=%async_computation | async-start | bytes 16384 | tf_op jit(solution)/shard_map/all_to_all | solution.py:125
  21.8 14.8 %copy-start.9 = (s32[64]{0:T(128)S(1)}, s32[64]{0:T(128)}, u32[]{:S(2)}) copy-start(s32[64]{0:T(128)} %param.14) | copy-start | bytes 772
  21.8 35.1 %copy-start.4 = (bf16[8,64,1024]{2,1,0:T(8,128)(2,1)S(1)}, bf16[8,64,1024]{2,1,0:T(8,128)(2,1)}, u32[]{:S(2)}) copy-start(bf16[8,64,1024]{2,1,0:T(8,128)(2,1)} %param.19) | copy-start | bytes 3145732
  21.8 64.7 %all-to-all-start.1 = ((bf16[16,2,1024,64]{2,3,1,0:T(8,128)(2,1)}), bf16[16,2,1024,64]{2,3,1,0:T(8,128)(2,1)}, u32[]{:S(2)}, u32[]{:S(2)}) async-start(bf16[16,2,1024,64]{2,3,1,0:T(8,128)(2,1)} %bitcast.125), calls=%async_computation.1 | async-start | bytes 8388608 | tf_op jit(solution)/shard_map/all_to_all | solution.py:128
  26.5 10.1 %collective-permute-start = (bf16[64,4,1024]{2,1,0:T(4,128)(2,1)}, bf16[64,4,1024]{2,1,0:T(4,128)(2,1)}, u32[]{:S(2)}, u32[]{:S(2)}) collective-permute-start(bf16[64,4,1024]{2,1,0:T(4,128)(2,1)} %param.11), channel_id=1, source_target_pairs={{0,1},{1,2},{2,3},{3,4},{4,5},{5,6},{6,7},{7,0},{8,9},{9,10},{10,1... | collective-permute-start | bytes 1572872 | tf_op jit(solution)/shard_map/ppermute | solution.py:156
  26.5 21.4 %collective-permute-start.4 = (bf16[64,4,1024]{2,1,0:T(4,128)(2,1)}, bf16[64,4,1024]{2,1,0:T(4,128)(2,1)}, u32[]{:S(2)}, u32[]{:S(2)}) collective-permute-start(bf16[64,4,1024]{2,1,0:T(4,128)(2,1)} %param.11), channel_id=1, source_target_pairs={{1,0},{2,1},{3,2},{4,3},{5,4},{6,5},{7,6},{0,7},{9,8},{10,9},{11,1... | collective-permute-start | bytes 1572872 | tf_op jit(solution)/shard_map/ppermute | solution.py:158
  36.6 10.1 %collective-permute-start.1 = (bf16[64,4,1024]{2,1,0:T(4,128)(2,1)}, bf16[64,4,1024]{2,1,0:T(4,128)(2,1)}, u32[]{:S(2)}, u32[]{:S(2)}) collective-permute-start(bf16[64,4,1024]{2,1,0:T(4,128)(2,1)} %collective-permute-done), channel_id=1, source_target_pairs={{0,1},{1,2},{2,3},{3,4},{4,5},{5,6},{6,7},{7,0},{8,9},{9,10},{10,1... | collective-permute-start | bytes 1572872 | tf_op jit(solution)/shard_map/ppermute | solution.py:156
  46.7 10.1 %collective-permute-start.2 = (bf16[64,4,1024]{2,1,0:T(4,128)(2,1)}, bf16[64,4,1024]{2,1,0:T(4,128)(2,1)}, u32[]{:S(2)}, u32[]{:S(2)}) collective-permute-start(bf16[64,4,1024]{2,1,0:T(4,128)(2,1)} %collective-permute-done.1), channel_id=1, source_target_pairs={{0,1},{1,2},{2,3},{3,4},{4,5},{5,6},{6,7},{7,0},{8,9},{9,10},{10,1... | collective-permute-start | bytes 1572872 | tf_op jit(solution)/shard_map/ppermute | solution.py:156
  47.9 43.9 %collective-permute-start.5 = (bf16[64,4,1024]{2,1,0:T(4,128)(2,1)}, bf16[64,4,1024]{2,1,0:T(4,128)(2,1)}, u32[]{:S(2)}, u32[]{:S(2)}) collective-permute-start(bf16[64,4,1024]{2,1,0:T(4,128)(2,1)} %collective-permute-done.4), channel_id=1, source_target_pairs={{1,0},{2,1},{3,2},{4,3},{5,4},{6,5},{7,6},{0,7},{9,8},{10,9},{11,1... | collective-permute-start | bytes 1572872 | tf_op jit(solution)/shard_map/ppermute | solution.py:158
  56.9 35.0 %collective-permute-start.3 = (bf16[64,4,1024]{2,1,0:T(4,128)(2,1)}, bf16[64,4,1024]{2,1,0:T(4,128)(2,1)}, u32[]{:S(2)}, u32[]{:S(2)}) collective-permute-start(bf16[64,4,1024]{2,1,0:T(4,128)(2,1)} %collective-permute-done.2), channel_id=1, source_target_pairs={{0,1},{1,2},{2,3},{3,4},{4,5},{5,6},{6,7},{7,0},{8,9},{9,10},{10,1... | collective-permute-start | bytes 1572872 | tf_op jit(solution)/shard_map/ppermute | solution.py:156
  86.5 89.4 %all-to-all-start.2 = ((bf16[16,2,64,1024]{3,2,1,0:T(8,128)(2,1)}), bf16[16,2,64,1024]{3,2,1,0:T(8,128)(2,1)}, u32[]{:S(2)}, u32[]{:S(2)}) async-start(bf16[16,2,64,1024]{3,2,1,0:T(8,128)(2,1)} %bitcast.126), calls=%async_computation.2 | async-start | bytes 8388608 | tf_op jit(solution)/shard_map/all_to_all | solution.py:129
  91.1 8.9 %copy-start.6 = (bf16[64,4,1024]{2,1,0:T(4,128)(2,1)S(1)}, bf16[64,4,1024]{2,1,0:T(4,128)(2,1)}, u32[]{:S(2)}) copy-start(bf16[64,4,1024]{2,1,0:T(4,128)(2,1)} %param.11) | copy-start | bytes 1572868
  91.8 13.2 %collective-permute-start.6 = (bf16[64,4,1024]{2,1,0:T(4,128)(2,1)}, bf16[64,4,1024]{2,1,0:T(4,128)(2,1)S(1)}, u32[]{:S(2)}, u32[]{:S(2)}) collective-permute-start(bf16[64,4,1024]{2,1,0:T(4,128)(2,1)} %collective-permute-done.5), channel_id=1, source_target_pairs={{1,0},{2,1},{3,2},{4,3},{5,4},{6,5},{7,6},{0,7},{9,8},{10,9},{11,1... | collective-permute-start | bytes 1572872 | tf_op jit(solution)/shard_map/ppermute | solution.py:158
  113.5 6.8 %copy-start.3 = (bf16[8,64,4,1024]{3,2,1,0:T(4,128)(2,1)S(1)}, bf16[8,64,4,1024]{3,2,1,0:T(4,128)(2,1)}, u32[]{:S(2)}) copy-start(bf16[8,64,4,1024]{3,2,1,0:T(4,128)(2,1)} %gather_fusion) | copy-start | bytes 12582916
  138.3 4.3 %copy-start.2 = (bf16[64,4,8192]{2,0,1:T(8,128)(2,1)S(1)}, bf16[64,4,8192]{2,0,1:T(8,128)(2,1)}, u32[]{:S(2)}) copy-start(bf16[64,4,8192]{2,0,1:T(8,128)(2,1)} %dot_general.37) | copy-start | bytes 12582916
  138.3 4.4 %copy-start.5 = (bf16[8192,128]{1,0:T(8,128)(2,1)S(1)}, bf16[8192,128]{1,0:T(8,128)(2,1)}, u32[]{:S(2)}) copy-start(bf16[8192,128]{1,0:T(8,128)(2,1)} %param.17) | copy-start | bytes 6291460
  143.9 2.9 %copy-start.7 = (bf16[8,32,1024,1]{2,1,0,3:T(8,128)(2,1)S(1)}, bf16[8,32,1024,1]{2,1,0,3:T(8,128)(2,1)}, u32[]{:S(2)}) copy-start(bf16[8,32,1024,1]{2,1,0,3:T(8,128)(2,1)} %reshape.505) | copy-start | bytes 1572868
  191.0 3.3 %copy-start.8 = (bf16[64,64,128]{2,1,0:T(8,128)(2,1)S(1)}, bf16[64,64,128]{2,1,0:T(8,128)(2,1)}, u32[]{:S(2)}) copy-start(bf16[64,64,128]{2,1,0:T(8,128)(2,1)} %param.20) | copy-start | bytes 3145732
  191.8 4.8 %copy-start.10 = (bf16[64,64,128]{2,1,0:T(8,128)(2,1)S(1)}, bf16[64,64,128]{2,1,0:T(8,128)(2,1)}, u32[]{:S(2)}) copy-start(bf16[64,64,128]{2,1,0:T(8,128)(2,1)} %param.21) | copy-start | bytes 3145732
  196.6 2.4 %copy-start.1 = (bf16[8192,128]{1,0:T(8,128)(2,1)S(1)}, bf16[8192,128]{1,0:T(8,128)(2,1)}, u32[]{:S(2)}) copy-start(bf16[8192,128]{1,0:T(8,128)(2,1)} %param.16) | copy-start | bytes 6291460
